TPU v7x, 32 devices: a whole 2x2x4 slice. The times are simulated.
32 devices in a mesh: grp: 2 (over core), ctx: 8 (over z, x), hd: 2 (over y).
Axes of the slice: x: 2, y: 2, z: 4, core: 2. Of those that a mesh axis runs over, the one named last changes fastest.
Arguments:
- video_q: bfloat16 [1024, 24, 128], P(('ctx', 'hd'), 'grp'), may hold values from -6 to 6
- video_k: bfloat16 [1024, 24, 128], P(('ctx', 'hd'), 'grp'), may hold values from -6 to 6
- video_v: bfloat16 [1024, 24, 128], P(('ctx', 'hd'), 'grp'), may hold values from -6 to 6
- positions: int32 [3, 1024], P(None, ('ctx', 'hd')), may hold values from 0 to 15, as said below
- text_q: bfloat16 [256, 24, 128], P(None, ('grp', 'hd')), may hold values from -16 to 16
- text_k: bfloat16 [256, 24, 128], P(None, ('grp', 'hd')), may hold values from -16 to 16
- text_v: bfloat16 [256, 24, 128], P(None, ('grp', 'hd')), may hold values from -6 to 6
- text_count: int32 [1], replicated, may hold values from 64 to 256
Outputs:
- video_out: bfloat16 [1024, 24, 128], P(('ctx', 'hd'), 'grp')
- text_out: bfloat16 [256, 24, 128], P('ctx', ('grp', 'hd'))
Inputs may be any that keep to these rules, and one draw needn't show every extreme that they name: `positions`: column n holds the frame, row and column of video token n; the columns are distinct cells of a grid of 4 frames of 16 by 16 cells.
All inputs are finite; a program needn't handle non-finite values.
Results may differ from a plain program's by a relative error of at most 0.0073.
Values may be sent and summed in bfloat16 or wider, within the bound.
A program may use at most 128 MiB of HBM per device.

v0:
```python
import math

import jax
import jax.numpy as jnp
from jax import lax
from jax.sharding import PartitionSpec as P

THETA = 256.0


def rotate(tokens_in, positions):
    head_dim = tokens_in.shape[-1]
    band_t = head_dim // 8
    band_h = (head_dim - band_t) // 2
    band_w = head_dim - band_t - band_h
    values = tokens_in.astype(jnp.float32)
    pieces = []
    offset = 0
    for axis_index, band_size in ((0, band_t), (1, band_h), (2, band_w)):
        half_size = band_size // 2
        frequency = THETA ** (-2.0 * jnp.arange(half_size, dtype=jnp.float32) / band_size)
        angles = positions[axis_index].astype(jnp.float32)[:, None] * frequency[None, :]
        cos_table = jnp.cos(angles)[:, None, :]
        sin_table = jnp.sin(angles)[:, None, :]
        lower_half = values[:, :, offset : offset + half_size]
        upper_half = values[:, :, offset + half_size : offset + band_size]
        pieces.append(lower_half * cos_table - upper_half * sin_table)
        pieces.append(upper_half * cos_table + lower_half * sin_table)
        offset += band_size
    return jnp.concatenate(pieces, axis=-1).astype(jnp.bfloat16)


def local(video_q, video_k, video_v, positions, text_q, text_k, text_v, text_count):
    rotated_q = rotate(video_q, positions)
    rotated_k = rotate(video_k, positions)
    queries_video, keys_video, values_video = (
        lax.all_to_all(rotated_q, "hd", split_axis=1, concat_axis=0, tiled=True),
        lax.all_to_all(rotated_k, "hd", split_axis=1, concat_axis=0, tiled=True),
        lax.all_to_all(video_v, "hd", split_axis=1, concat_axis=0, tiled=True),
    )
    cycle_size = lax.axis_size("ctx")
    text_share = text_q.shape[0] // cycle_size
    own_text = lax.dynamic_slice_in_dim(text_q, lax.axis_index("ctx") * text_share, text_share, 0)
    queries = jnp.concatenate([queries_video, own_text], axis=0)
    scale = 1.0 / math.sqrt(queries.shape[-1])
    text_live = jnp.arange(text_k.shape[0], dtype=jnp.int32) < text_count[0]
    scores = jnp.einsum("qhd,khd->qhk", queries, text_k, preferred_element_type=jnp.float32) * scale
    scores = jnp.where(text_live[None, None, :], scores, -jnp.inf)
    peak = jnp.max(scores, axis=2)
    probs = jnp.exp(scores - peak[..., None])
    total = jnp.sum(probs, axis=2)
    mixed = jnp.einsum(
        "qhk,khd->qhd", probs.astype(jnp.bfloat16), text_v, preferred_element_type=jnp.float32
    )
    keys_all, values_all = (
        lax.all_gather(keys_video, "ctx", axis=0, tiled=True),
        lax.all_gather(values_video, "ctx", axis=0, tiled=True),
    )
    piece_scores = (
        jnp.einsum("qhd,khd->qhk", queries, keys_all, preferred_element_type=jnp.float32) * scale
    )
    new_peak = jnp.maximum(peak, jnp.max(piece_scores, axis=2))
    factor = jnp.exp(peak - new_peak)
    piece_probs = jnp.exp(piece_scores - new_peak[..., None])
    new_total = total * factor + jnp.sum(piece_probs, axis=2)
    new_mixed = mixed * factor[..., None] + jnp.einsum(
        "qhk,khd->qhd",
        piece_probs.astype(jnp.bfloat16),
        values_all,
        preferred_element_type=jnp.float32,
    )
    attended = (new_mixed / new_total[..., None]).astype(jnp.bfloat16)
    video_rows = queries_video.shape[0]
    video_heads = attended[:video_rows]
    text_out = attended[video_rows:]
    video_out = lax.all_to_all(video_heads, "hd", split_axis=0, concat_axis=1, tiled=True)
    return (video_out, text_out)


def solution(mesh):
    return jax.shard_map(
        local,
        mesh=mesh,
        in_specs=(
            P(("ctx", "hd"), "grp", None),
            P(("ctx", "hd"), "grp", None),
            P(("ctx", "hd"), "grp", None),
            P(None, ("ctx", "hd")),
            P(None, ("grp", "hd"), None),
            P(None, ("grp", "hd"), None),
            P(None, ("grp", "hd"), None),
            P(),
        ),
        out_specs=(P(("ctx", "hd"), "grp", None), P("ctx", ("grp", "hd"), None)),
        check_vma=False,
    )
```

profile of v0, /device:TPU:0, one launch (start us, length us, event | category | flops | bytes accessed | tf_op | source)
XLA Modules:
  0.0 131.7 jit_solution(14580065879339598810)
XLA Ops:
  7.2 0.0 copy-start
  7.2 0.0 all-gather.3.cloned.1.call-start
  7.3 0.8 convert_bitcast_fusion
  8.1 1.0 convert_element_type.58
  9.0 0.1 multiply_cosine_fusion.2
  9.1 0.1 copy.19
  9.2 0.1 copy.20
  9.3 0.0 copy-start.3
  9.3 1.0 convert_element_type.50
  10.3 0.3 multiply_cosine_fusion
  10.6 0.4 add_convert_fusion.2
  11.0 0.5 add_convert_fusion
  11.5 0.6 concatenate.13
  12.1 8.9 %all_to_all.72 = bf16[64,12,128]{2,0,1:T(8,128)(2,1)S(1)} all-to-all(bf16[64,12,128]{2,0,1:T(8,128)(2,1)S(1)} %concatenate.13), channel_id=1, replica_groups=mesh['grp'=2,'ctx'=8,'hd'=2] {'hd'}, dimensions={1} | all-to-all | bytes 393216 | tf_op jit(solution)/shard_map/all_to_all | solution.py:38
  20.9 0.7 copy.22
  21.6 0.0 all-gather.3.cloned.1.call-update
  21.6 0.0 all-gather.5.cloned.1.call-start
  21.7 0.0 copy-done.3
  21.7 7.2 %all_to_all.73 = bf16[64,12,128]{2,0,1:T(8,128)(2,1)S(1)} all-to-all(bf16[64,12,128]{2,0,1:T(8,128)(2,1)S(1)} %copy-done.3), channel_id=1, replica_groups=mesh['grp'=2,'ctx'=8,'hd'=2] {'hd'}, dimensions={1} | all-to-all | bytes 393216 | tf_op jit(solution)/shard_map/all_to_all | solution.py:39
  28.9 0.7 copy.23
  29.6 0.0 all-gather.5.cloned.1.call-update
  29.6 0.5 add_convert_fusion.3
  30.1 1.2 concatenate.11
  31.3 3.4 %all-to-all-start = ((bf16[64,12,128]{2,0,1:T(8,128)(2,1)}), bf16[64,12,128]{2,0,1:T(8,128)(2,1)S(1)}, u32[]{:S(2)}, u32[]{:S(2)}) async-start(bf16[64,12,128]{2,0,1:T(8,128)(2,1)} %concatenate.11), calls=%async_computation | async-start | bytes 393216 | tf_op jit(solution)/shard_map/all_to_all | solution.py:37
  35.4 0.8 constant_dynamic-slice_fusion
  36.2 3.3 %all-to-all-done = bf16[64,12,128]{2,0,1:T(8,128)(2,1)S(1)} async-done(((bf16[64,12,128]{2,0,1:T(8,128)(2,1)}), bf16[64,12,128]{2,0,1:T(8,128)(2,1)S(1)}, u32[]{:S(2)}, u32[]{:S(2)}) %all-to-all-start) | async-done | bytes 196640 | tf_op jit(solution)/shard_map/all_to_all | solution.py:37
  39.6 0.0 copy-done
  39.6 0.5 fusion.30
  40.1 0.5 fusion.22
  40.5 0.0 copy-start.2
  40.6 25.8 %all-gather.3.cloned.1.call-done = bf16[1024,6,128]{2,0,1:T(8,128)(2,1)} async-done(((bf16[128,6,128]{2,0,1:T(8,128)(2,1)}), bf16[1024,6,128]{2,0,1:T(8,128)(2,1)}) %all-gather.3.cloned.1.call-update) | async-done | bytes 1572880 | tf_op jit(solution)/shard_map/all_gather | solution.py:56
  66.3 2.2 %bitcast_reduce_fusion = (f32[160,6]{0,1:T(8,128)S(1)}, f32[6,1024,160]{1,2,0:T(8,128)S(1)}) fusion(bf16[1024,6,128]{2,0,1:T(8,128)(2,1)} %all-gather.3.cloned.1.call-done, bf16[32,6,128]{2,0,1:T(8,128)(2,1)S(1)} %constant_dynamic-slice_fusion, bf16[128,6,128]{2,0,1:T(8,128)(2,1)S(1)} %bitcast.61), kind=kOutput, calls=%fused_computation.1 | convolution fusion | flops 254114880 | bytes 5754624 | tf_op jit(solution)/shard_map/qhd,khd->qhk/dot_general | solution.py:60
  68.5 0.0 copy-start.1
  68.5 1.9 %copy-done.1 = f32[6,1024,160]{1,2,0:T(8,128)} copy-done((f32[6,1024,160]{1,2,0:T(8,128)}, f32[6,1024,160]{1,2,0:T(8,128)S(1)}, u32[]{:S(2)}) %copy-start.1) | copy-done | bytes 3932184
  70.4 0.9 fusion.1
  71.3 0.0 copy-done.2
  71.3 0.4 fusion.15
  71.6 39.4 %all-gather.5.cloned.1.call-done = bf16[1024,6,128]{2,0,1:T(8,128)(2,1)} async-done(((bf16[128,6,128]{2,0,1:T(8,128)(2,1)}), bf16[1024,6,128]{2,0,1:T(8,128)(2,1)}) %all-gather.5.cloned.1.call-update) | async-done | bytes 1572880 | tf_op jit(solution)/shard_map/all_gather | solution.py:57
  111.1 3.6 %fusion.19 = bf16[160,6,128]{2,0,1:T(8,128)(2,1)S(1)} fusion(f32[160,6,128]{2,0,1:T(8,128)S(1)} %fusion.15, bf16[1024,6,128]{2,0,1:T(8,128)(2,1)} %all-gather.5.cloned.1.call-done, f32[6,1024,160]{1,2,0:T(8,128)} %copy-done.1, f32[160,6]{0,1:T(8,128)S(1)} %max.13, f32[160,6]{0,1:T(8,128)S(1)} %get-tuple-element.2), kind=kOutput, calls=%fused_computation.16 | convolution fusion | flops 254976000 | bytes 6249984 | tf_op jit(solution)/shard_map/qhk,khd->qhd/dot_general | solution.py:66
  114.7 0.8 copy.24
  115.5 3.4 %all-to-all-start.3 = ((bf16[128,6,128]{2,1,0:T(8,128)(2,1)}), bf16[128,6,128]{2,1,0:T(8,128)(2,1)S(1)}, u32[]{:S(2)}, u32[]{:S(2)}) async-start(bf16[128,6,128]{2,1,0:T(8,128)(2,1)} %copy.24), calls=%async_computation.3 | async-start | bytes 524288 | tf_op jit(solution)/shard_map/all_to_all | solution.py:76
  119.0 0.6 slice.84
  119.6 4.5 %all-to-all-done.3 = bf16[128,6,128]{2,1,0:T(8,128)(2,1)S(1)} async-done(((bf16[128,6,128]{2,1,0:T(8,128)(2,1)}), bf16[128,6,128]{2,1,0:T(8,128)(2,1)S(1)}, u32[]{:S(2)}, u32[]{:S(2)}) %all-to-all-start.3) | async-done | bytes 196640 | tf_op jit(solution)/shard_map/all_to_all | solution.py:76
  124.1 0.7 copy.25
  (7 shorter events, 0.1 us)
Async XLA Ops:
  7.2 32.4 %copy-start = (bf16[256,6,128]{2,0,1:T(8,128)(2,1)S(1)}, bf16[256,6,128]{2,0,1:T(8,128)(2,1)}, u32[]{:S(2)}) copy-start(bf16[256,6,128]{2,0,1:T(8,128)(2,1)} %param.13) | copy-start | bytes 1179652
  7.2 59.1 %all-gather.3.cloned.1.call-start = ((), (), s32[]{:S(2)}) async-start(), calls=%async_computation.4 | async-start | bytes 1769472 | tf_op jit(solution)/shard_map/all_gather | solution.py:56
  9.3 12.4 %copy-start.3 = (bf16[64,12,128]{2,0,1:T(8,128)(2,1)S(1)}, bf16[64,12,128]{2,0,1:T(8,128)(2,1)}, u32[]{:S(2)}) copy-start(bf16[64,12,128]{2,0,1:T(8,128)(2,1)} %param.10) | copy-start | bytes 589828
  21.6 89.4 %all-gather.5.cloned.1.call-start = ((), (), s32[]{:S(2)}) async-start(), calls=%async_computation.5 | async-start | bytes 1769472 | tf_op jit(solution)/shard_map/all_gather | solution.py:57
  31.3 8.2 %all-to-all-start = ((bf16[64,12,128]{2,0,1:T(8,128)(2,1)}), bf16[64,12,128]{2,0,1:T(8,128)(2,1)S(1)}, u32[]{:S(2)}, u32[]{:S(2)}) async-start(bf16[64,12,128]{2,0,1:T(8,128)(2,1)} %concatenate.11), calls=%async_computation | async-start | bytes 393216 | tf_op jit(solution)/shard_map/all_to_all | solution.py:37
  40.5 30.7 %copy-start.2 = (bf16[256,6,128]{2,0,1:T(8,128)(2,1)S(1)}, bf16[256,6,128]{2,0,1:T(8,128)(2,1)}, u32[]{:S(2)}) copy-start(bf16[256,6,128]{2,0,1:T(8,128)(2,1)} %param.14) | copy-start | bytes 1179652
  68.5 1.9 %copy-start.1 = (f32[6,1024,160]{1,2,0:T(8,128)}, f32[6,1024,160]{1,2,0:T(8,128)S(1)}, u32[]{:S(2)}) copy-start(f32[6,1024,160]{1,2,0:T(8,128)S(1)} %get-tuple-element.36) | copy-start | bytes 11796484
  115.5 8.6 %all-to-all-start.3 = ((bf16[128,6,128]{2,1,0:T(8,128)(2,1)}), bf16[128,6,128]{2,1,0:T(8,128)(2,1)S(1)}, u32[]{:S(2)}, u32[]{:S(2)}) async-start(bf16[128,6,128]{2,1,0:T(8,128)(2,1)} %copy.24), calls=%async_computation.3 | async-start | bytes 524288 | tf_op jit(solution)/shard_map/all_to_all | solution.py:76
Sparse Core Ops, SparseCore 0:
  21.8 44.4 all-gather.2
  68.5 42.5 all-gather.4
where the time goes:
time: 132 us
  waiting for transfers between devices  73.1 us (55%)
  blocking collectives  16.1 us (12%)
  between operations  14.8 us (11%)
  local copies, waits for them, and re-layouts  8.23 us (6%)
  starting transfers between devices  6.95 us (5%)
  matrix products  6.57 us (5%)
  other arithmetic  5.87 us (4%)
    all_gather x1, waiting for transfers between devices, local(): lax.all_gather(values_video, 'ctx', axis=0, tiled=True)  39.4 us
    all_gather x1, waiting for transfers between devices, local(): lax.all_gather(keys_video, 'ctx', axis=0, tiled=True)  25.8 us
    all_to_all x1, blocking collectives, local(): lax.all_to_all(rotated_k, 'hd', split_axis=1, concat_axis=0, tiled=True)  8.89 us
    all_to_all x1, blocking collectives, local(): lax.all_to_all(video_v, 'hd', split_axis=1, concat_axis=0, tiled=True)  7.21 us
    all_to_all x1, waiting for transfers between devices, local(): lax.all_to_all(video_heads, 'hd', split_axis=0, concat_axis=1, tiled=True)  4.53 us
    dot_general x1, matrix products, local(): jnp.einsum('qhk,khd->qhd', piece_probs.astype(jnp.bfloat16), values_all,...  3.56 us
    all_to_all x1, starting transfers between devices, local(): lax.all_to_all(video_heads, 'hd', split_axis=0, concat_axis=1, tiled=True)  3.44 us
    all_to_all x1, starting transfers between devices, local(): lax.all_to_all(rotated_q, 'hd', split_axis=1, concat_axis=0, tiled=True)  3.43 us
  transfers between devices with their start and end apart: 4, of which 4 were waited for; matrix products, arithmetic and copies ran while one was open for 6% of the time, Pallas kernels for 0%

commit v1 on v0

v1 whole, which is shorter than its diff:
```python
import functools
import math

import jax
import jax.numpy as jnp
import numpy as np
from jax import lax
from jax.experimental import pallas as pl
from jax.experimental.pallas import tpu as pltpu
from jax.sharding import PartitionSpec as P

THETA = 256.0
MESH = pl.DeviceIdType.MESH
PAIR = 2
NEAR = 2


def bands(dim):
    band_t = dim // 8
    band_h = (dim - band_t) // 2
    return (band_t, band_h, dim - band_t - band_h)


def constants(dim):
    axis = np.zeros((dim,), np.int32)
    freq = np.zeros((dim,), np.float32)
    swap = np.zeros((dim, dim), np.float32)
    start = 0
    for index, size in enumerate(bands(dim)):
        half = size // 2
        for i in range(half):
            low, high = start + i, start + half + i
            axis[low] = axis[high] = index
            freq[low] = freq[high] = np.float32(THETA ** (-2.0 * i / size))
            swap[high, low] = -1.0
            swap[low, high] = 1.0
        start += size
    return axis, freq, swap


def each(count, body):
    if count <= 4:
        for i in range(count):
            body(i)
    else:
        lax.fori_loop(0, count, lambda i, _: (body(i), 0)[1], 0)


def kernel(far, hds, q_ref, k_ref, v_ref, cos_ref, sin_ref, swap_ref, tq_ref, tk_ref, tv_ref, count_ref,
           out_ref, tout_ref, qs, ks, qg, kv, ost, tst, acc, peak, total,
           a_send, q_recv, kv_recv, f_send, n_send, o_send, o_recv, t_sems):
    ctx = lax.axis_index("ctx")
    hd = lax.axis_index("hd")
    fi, mi, ni = ctx // (PAIR * NEAR), (ctx // NEAR) % PAIR, ctx % NEAR
    groups = PAIR * hds
    heads = v_ref.shape[1]
    tokens, dim = v_ref.shape[2], v_ref.shape[3]
    mine = hd * PAIR + mi
    slot = fi * NEAR + ni

    def at(f, m, n, h):
        return {"ctx": (f * PAIR + m) * NEAR + n, "hd": h}

    def group_peer(d):
        g = lax.rem(mine + d, groups)
        return g, at(fi, g % PAIR, ni, g // PAIR)

    def far_peer(d):
        f = lax.rem(fi + d, far)
        return f, at(f, mi, ni, hd)

    def near_peer(d):
        n = lax.rem(ni + d, NEAR)
        return n, at(fi, mi, n, hd)

    barrier = pltpu.get_barrier_semaphore()

    def greet(peer):
        pl.semaphore_signal(barrier, inc=1, device_id=peer, device_id_type=MESH)

    each(groups - 1, lambda i: greet(group_peer(i + 1)[1]))
    each(far - 1, lambda i: greet(far_peer(i + 1)[1]))
    each(NEAR - 1, lambda i: greet(near_peer(i + 1)[1]))

    cos, sin, swap = cos_ref[...], sin_ref[...], swap_ref[...]

    def rotate(src, dst):
        for g in range(groups):
            for h in range(heads):
                x = src[g, h]
                turned = jnp.dot(x, swap, preferred_element_type=jnp.float32)
                dst[g, h] = (x.astype(jnp.float32) * cos + turned * sin).astype(jnp.bfloat16)

    rotate(k_ref, ks)
    rotate(q_ref, qs)
    kv[slot, 0, mine] = ks[mine]
    kv[slot, 1, mine] = v_ref[mine]
    qg[mine] = qs[mine]
    pl.semaphore_wait(barrier, (groups - 1) + (far - 1) + (NEAR - 1))

    def remote(src, dst, send, recv, peer):
        return pltpu.make_async_remote_copy(src_ref=src, dst_ref=dst, send_sem=send, recv_sem=recv,
                                            device_id=peer, device_id_type=MESH)

    def kv_to_group(w, d):
        g, peer = group_peer(d)
        src = ks if w == 0 else v_ref
        return remote(src.at[g], kv.at[slot, w, mine], a_send.at[w, d], kv_recv.at[slot, w, mine], peer)

    def q_to_group(d):
        g, peer = group_peer(d)
        return remote(qs.at[g], qg.at[mine], a_send.at[2, d], q_recv.at[mine], peer)

    def kv_to_far(w, g, d):
        f, peer = far_peer(d)
        piece = kv.at[slot, w, g]
        return remote(piece, piece, f_send.at[d, w, g], kv_recv.at[slot, w, g], peer)

    def kv_to_near(s, w, g, d):
        n, peer = near_peer(d)
        piece = kv.at[s, w, g]
        return remote(piece, piece, n_send.at[s // NEAR, w, g], kv_recv.at[s, w, g], peer)

    def arrived(s, w, g):
        piece = kv.at[s, w, g]
        remote(piece, piece, n_send.at[0, w, g], kv_recv.at[s, w, g], near_peer(1)[1]).wait_recv()

    def spread(w, g):
        each(far - 1, lambda i: kv_to_far(w, g, i + 1).start())
        kv_to_near(slot, w, g, 1).start()

    for w in range(2):
        for d in range(1, groups):
            kv_to_group(w, d).start()
        spread(w, mine)
        if w == 0:
            for d in range(1, groups):
                q_to_group(d).start()
    for w in range(2):
        for d in range(1, groups):
            g = lax.rem(mine + d, groups)
            arrived(slot, w, g)
            spread(w, g)

    scale = math.log2(math.e) / math.sqrt(dim)
    rows = groups * tokens

    def queries(h):
        return jnp.concatenate([qg[:, h].reshape(rows, dim), tq_ref[h]], axis=0)

    def score(h, keys):
        return lax.dot_general(queries(h), keys, (((1,), (1,)), ((), ())), preferred_element_type=jnp.float32) * scale

    for d in range(1, groups):
        g = lax.rem(mine + d, groups)
        remote(qg.at[g], qg.at[g], a_send.at[2, d], q_recv.at[g], group_peer(d)[1]).wait_recv()

    for h in range(heads):
        s = score(h, tk_ref[h])
        live = lax.broadcasted_iota(jnp.int32, s.shape, 1) < count_ref[0]
        s = jnp.where(live, s, -jnp.inf)
        top = jnp.max(s, axis=1, keepdims=True)
        p = jnp.exp2(s - top)
        peak[h] = top
        total[h] = jnp.sum(p, axis=1, keepdims=True)
        acc[h] = jnp.dot(p.astype(jnp.bfloat16), tv_ref[h], preferred_element_type=jnp.float32)

    def absorb(h, s):
        keys = kv[s, 0, :, h].reshape(rows, dim)
        values = kv[s, 1, :, h].reshape(rows, dim)
        sc = score(h, keys)
        old = peak[h]
        top = jnp.maximum(old, jnp.max(sc, axis=1, keepdims=True))
        p = jnp.exp2(sc - top)
        factor = jnp.exp2(old - top)
        peak[h] = top
        total[h] = total[h] * factor + jnp.sum(p, axis=1, keepdims=True)
        acc[h] = acc[h] * factor + jnp.dot(p.astype(jnp.bfloat16), values, preferred_element_type=jnp.float32)

    for h in range(heads):
        absorb(h, slot)

    def relay(i):
        s = far_peer(i + 1)[0] * NEAR + ni
        for w in range(2):
            for d in range(groups):
                g = lax.rem(mine + d, groups)
                arrived(s, w, g)
                kv_to_near(s, w, g, 1).start()
    each(far - 1, relay)

    other = near_peer(1)[0]

    def take(s):
        for w in range(2):
            for d in range(groups):
                arrived(s, w, lax.rem(mine + d, groups))

    near_slot = fi * NEAR + other
    take(near_slot)
    for h in range(heads):
        absorb(h, near_slot)

    def from_far(i):
        for h in range(heads):
            absorb(h, far_peer(i + 1)[0] * NEAR + ni)
    each(far - 1, from_far)

    def across(i):
        s = far_peer(i + 1)[0] * NEAR + other
        take(s)
        for h in range(heads):
            absorb(h, s)
    each(far - 2, across)
    last = far_peer(far - 1)[0] * NEAR + other
    take(last)

    def out_to(h, d):
        g, peer = group_peer(d)
        return remote(ost.at[h, g], out_ref.at[mine, h], o_send.at[h, d], o_recv.at[h, mine], peer)

    partner = lax.rem(mi + 1, PAIR)

    def text_to(h):
        return remote(tst.at[h, partner], tout_ref.at[mi, h], t_sems.at[0, h], t_sems.at[1, h],
                      at(fi, partner, ni, hd))

    for h in range(heads):
        absorb(h, last)
        result = (acc[h] / total[h]).astype(jnp.bfloat16)
        ost[h] = result[:rows].reshape(groups, tokens, dim)
        tst[h] = result[rows:].reshape(tst.shape[1:])
        for d in range(1, groups):
            out_to(h, d).start()
        text_to(h).start()
        out_ref[mine, h] = ost[h, mine]
        tout_ref[mi, h] = tst[h, mi]

    for d in range(1, groups):
        kv_to_group(0, d).wait_send()
        kv_to_group(1, d).wait_send()
        q_to_group(d).wait_send()
    for w in range(2):
        for d in range(groups):
            g = lax.rem(mine + d, groups)
            each(far - 1, lambda i: kv_to_far(w, g, i + 1).wait_send())
            each(far, lambda i: kv_to_near(far_peer(i)[0] * NEAR + ni, w, g, 1).wait_send())
    for h in range(heads):
        for d in range(1, groups):
            g, peer = group_peer(d)
            out_to(h, d).wait_send()
            remote(ost.at[h, g], out_ref.at[g, h], o_send.at[h, d], o_recv.at[h, g], peer).wait_recv()
        text_to(h).wait_send()
        remote(tst.at[h, partner], tout_ref.at[partner, h], t_sems.at[0, h], t_sems.at[1, h],
               at(fi, partner, ni, hd)).wait_recv()


def local(ctxs, hds, video_q, video_k, video_v, positions, text_q, text_k, text_v, text_count):
    tokens, all_heads, dim = video_q.shape
    text = text_q.shape[0]
    groups = PAIR * hds
    heads = all_heads // groups
    far = ctxs // (PAIR * NEAR)
    share = text // ctxs
    rows = groups * tokens + PAIR * share
    axis, freq, swap = constants(dim)
    pos = positions.astype(jnp.float32)[:, :, None]
    lane_axis = axis[None, :]
    angle = jnp.where(lane_axis == 0, pos[0], jnp.where(lane_axis == 1, pos[1], pos[2])) * freq[None, :]
    cos, sin = jnp.cos(angle), jnp.sin(angle)

    def by_head(x):
        return jnp.swapaxes(x, 0, 1).reshape(groups, heads, tokens, dim)

    ctx = lax.axis_index("ctx")
    fi, mi, ni = ctx // (PAIR * NEAR), (ctx // NEAR) % PAIR, ctx % NEAR

    def text_heads(x):
        return jnp.swapaxes(lax.dynamic_slice_in_dim(x, mi * heads, heads, 1), 0, 1)

    tq = text_q.reshape(far, PAIR, NEAR, share, PAIR * heads, dim)
    tq = lax.dynamic_slice(tq, (fi, 0, ni, 0, mi * heads, 0), (1, PAIR, 1, share, heads, dim))
    tq = jnp.swapaxes(tq.reshape(PAIR * share, heads, dim), 0, 1)
    vmem = pl.BlockSpec(memory_space=pltpu.VMEM)
    dma = pltpu.SemaphoreType.DMA
    slots = far * NEAR
    out, tout = pl.pallas_call(
        functools.partial(kernel, far, hds),
        name="joint_attention",
        out_shape=(
            jax.ShapeDtypeStruct((groups, heads, tokens, dim), jnp.bfloat16),
            jax.ShapeDtypeStruct((PAIR, heads, share, dim), jnp.bfloat16),
        ),
        in_specs=[vmem] * 9 + [pl.BlockSpec(memory_space=pltpu.SMEM)],
        out_specs=(vmem, vmem),
        scratch_shapes=[
            pltpu.VMEM((groups, heads, tokens, dim), jnp.bfloat16),
            pltpu.VMEM((groups, heads, tokens, dim), jnp.bfloat16),
            pltpu.VMEM((groups, heads, tokens, dim), jnp.bfloat16),
            pltpu.VMEM((slots, 2, groups, heads, tokens, dim), jnp.bfloat16),
            pltpu.VMEM((heads, groups, tokens, dim), jnp.bfloat16),
            pltpu.VMEM((heads, PAIR, share, dim), jnp.bfloat16),
            pltpu.VMEM((heads, rows, dim), jnp.float32),
            pltpu.VMEM((heads, rows, 1), jnp.float32),
            pltpu.VMEM((heads, rows, 1), jnp.float32),
            dma((3, groups)),
            dma((groups,)),
            dma((slots, 2, groups)),
            dma((far, 2, groups)),
            dma((far, 2, groups)),
            dma((heads, groups)),
            dma((heads, groups)),
            dma((2, heads)),
        ],
        compiler_params=pltpu.CompilerParams(
            collective_id=0, has_side_effects=True, vmem_limit_bytes=60 * 1024 * 1024
        ),
    )(
        by_head(video_q), by_head(video_k), by_head(video_v), cos, sin, jnp.asarray(swap, jnp.bfloat16),
        tq, text_heads(text_k), text_heads(text_v), text_count,
    )
    video_out = jnp.swapaxes(out.reshape(all_heads, tokens, dim), 0, 1)
    text_out = jnp.swapaxes(tout.reshape(PAIR * heads, share, dim), 0, 1)
    return (video_out, text_out)


def solution(mesh):
    return jax.shard_map(
        functools.partial(local, mesh.shape["ctx"], mesh.shape["hd"]),
        mesh=mesh,
        in_specs=(
            P(("ctx", "hd"), "grp", None),
            P(("ctx", "hd"), "grp", None),
            P(("ctx", "hd"), "grp", None),
            P(None, ("ctx", "hd")),
            P(None, ("grp", "hd"), None),
            P(None, ("grp", "hd"), None),
            P(None, ("grp", "hd"), None),
            P(),
        ),
        out_specs=(P(("ctx", "hd"), "grp", None), P("ctx", ("grp", "hd"), None)),
        check_vma=False,
    )
```

time: 132 us -> 49.1 us (0.37)
  waiting for transfers between devices: 73.1 us -> 0 us
  Pallas kernels: 0 us -> 40.3 us
  blocking collectives: 16.1 us -> 0 us
  between operations: 14.8 us -> 1.4 us
  starting transfers between devices: 6.95 us -> 0 us
  matrix products: 6.57 us -> 0 us
  other arithmetic: 5.87 us -> 0.85 us
  local copies, waits for them, and re-layouts: 8.23 us -> 6.3 us
    all_gather x2 -> x0, waiting for transfers between devices: 65.2 us -> none  [the longest x1 39.4 us: local(): lax.all_gather(values_video, 'ctx', axis=0, tiled=True)]
    pallas_call x0 -> x1, Pallas kernels: none -> 40.3 us  [local(): pl.pallas_call(functools.partial(kernel, far, hds), name='joint_attention...]
    all_to_all x2 -> x0, blocking collectives: 16.1 us -> none  [the longest x1 8.89 us: local(): lax.all_to_all(rotated_k, 'hd', split_axis=1, concat_axis=0, tiled=True)]
    all_to_all x2 -> x0, waiting for transfers between devices: 7.87 us -> none  [the longest x1 4.53 us: local(): lax.all_to_all(video_heads, 'hd', split_axis=0, concat_axis=1, tiled=True)]
    all_to_all x2 -> x0, starting transfers between devices: 6.87 us -> none  [the longest x1 3.44 us: local(): lax.all_to_all(video_heads, 'hd', split_axis=0, concat_axis=1, tiled=True)]
    dot_general x4 -> x0, matrix products: 6.57 us -> none  [the longest x1 3.56 us: local(): jnp.einsum('qhk,khd->qhd', piece_probs.astype(jnp.bfloat16), values_all,...]
    convert_element_type x3 -> x1, other arithmetic: 2.75 us -> 0.01 us  [local(): pos = positions.astype(jnp.float32)[:, :, None]]
    all_to_all x4 -> x0, local copies, waits for them, and re-layouts: 2.09 us -> none  [the longest x1 0.71 us: local(): lax.all_to_all(video_heads, 'hd', split_axis=0, concat_axis=1, tiled=True)]
  transfers between devices with their start and end apart: 4 -> 0, of which waited for: 4 -> 0; matrix products, arithmetic and copies ran while one was open for 6% -> 0% of each run, Pallas kernels for 0% -> 0%
where the time goes in v1:
time: 49.1 us; the launch traced here: 48.8 us
  Pallas kernels  40.3 us (82%)
  local copies, waits for them, and re-layouts  6.3 us (13%)
  between operations  1.4 us (3%)
  other arithmetic  0.85 us (2%)
    pallas_call x1, Pallas kernels, local(): pl.pallas_call(functools.partial(kernel, far, hds), name='joint_attention...  40.3 us
    unnamed x14, local copies, waits for them, and re-layouts  3.89 us
    transpose x1, local copies, waits for them, and re-layouts, text_heads(): return jnp.swapaxes(lax.dynamic_slice_in_dim(x, mi * heads, heads, 1), 0, 1)  1.78 us

profile of v1, /device:TPU:0, one launch (start us, length us, event | category | flops | bytes accessed | tf_op | source)
XLA Modules:
  0.0 48.8 jit_solution(17922449604006523663)
XLA Ops:
  0.6 0.0 copy-start
  1.4 0.3 copy-done
  1.6 0.0 copy-start.2
  1.7 0.7 %copy-done.2 = s32[3,64]{1,0:T(4,128)S(1)} copy-done((s32[3,64]{1,0:T(4,128)S(1)}, s32[3,64]{1,0:T(4,128)}, u32[]{:S(2)}) %copy-start.2) | copy-done | bytes 792
  2.3 0.6 %constant_dynamic-slice_fusion = bf16[1,2,1,32,3,128]{5,3,2,1,0,4:T(8,128)(2,1)} fusion(bf16[2,2,2,32,6,128]{5,3,2,1,0,4:T(8,128)(2,1)S(1)} %bitcast.31, s32[]{:T(128)S(6)} %select_n.40, s32[]{:T(128)S(6)} %select_n.42, s32[]{:T(128)S(6)} %select_n.45), kind=kLoop, calls=%fused_computation.5 | loop fusion | bytes 98316 | tf_op jit(solution)/shard_map/dynamic_slice | solution.py:282
  3.0 0.0 copy-start.3
  3.0 0.0 copy-start.4
  3.0 0.0 copy-start.5
  3.0 0.6 %copy-done.3 = f32[128]{0:T(128)S(1)} copy-done((f32[128]{0:T(128)S(1)}, f32[128]{0:T(128)}, u32[]{:S(2)}) %copy-start.3) | copy-done | bytes 536
  3.6 0.0 copy-done.4
  3.6 0.0 copy-done.5
  3.7 0.8 %fusion = (f32[64,128]{1,0:T(8,128)}, f32[64,128]{1,0:T(8,128)}) fusion(f32[128]{0:T(128)S(1)} %copy-done.3, f32[64]{0:T(128)S(1)} %get-tuple-element.9, f32[64]{0:T(128)S(1)} %get-tuple-element.10, f32[64]{0:T(128)S(1)} %get-tuple-element.8, pred[128]{0:T(512)(128)(4,1)S(1)} %copy-done.4, pred[128]{0:T(512)(128)(4,1)S(1)} %copy-done.5), kind=kLoop, calls=%fused_computation.3 | loop fusion | flops 24576 | bytes 67072 | tf_op jit(solution)/shard_map/sin | solution.py:270
  4.5 1.8 %dynamic-slice_bitcast_fusion = (bf16[3,256,128]{2,1,0:T(8,128)(2,1)}, bf16[3,256,128]{2,1,0:T(8,128)(2,1)}) fusion(bf16[256,6,128]{2,0,1:T(8,128)(2,1)} %param.18, s32[]{:T(128)S(6)} %select_n.45, bf16[256,6,128]{2,0,1:T(8,128)(2,1)} %param.17), kind=kLoop, calls=%fused_computation | loop fusion | bytes 786436 | tf_op jit(solution)/shard_map/transpose | solution.py:279
  6.3 40.3 %joint_attention.1 = (bf16[4,3,64,128]{3,2,1,0:T(8,128)(2,1)}, bf16[2,3,32,128]{3,2,1,0:T(8,128)(2,1)}) custom-call(bf16[4,3,64,128]{3,2,1,0:T(8,128)(2,1)} %bitcast.34, bf16[4,3,64,128]{3,2,1,0:T(8,128)(2,1)} %bitcast.35, bf16[4,3,64,128]{3,2,1,0:T(8,128)(2,1)} %bitcast.36, f32[64,128]{1,0:T(8,128)} %get-tuple-element.7.cos_ref, ...), custom_call_target="tpu_custom_call" | custom-call | tf_op jit(solution)/shard_map/joint_attention/pallas_call | solution.py:287
  46.6 0.0 copy-start.1
  46.6 1.6 %copy.19 = bf16[64,12,128]{2,0,1:T(8,128)(2,1)} copy(bf16[64,12,128]{2,0,1:T(8,128)(2,1)} %bitcast.33) | data formatting | bytes 393216
  48.2 0.0 copy-done.1
  48.2 0.6 %copy.20 = bf16[32,6,128]{2,0,1:T(8,128)(2,1)} copy(bf16[32,6,128]{2,0,1:T(8,128)(2,1)S(1)} %bitcast.37) | data formatting | bytes 98304
  (2 shorter events, 0.0 us)
Async XLA Ops:
  0.6 1.0 %copy-start = (bf16[256,6,128]{2,0,1:T(8,128)(2,1)S(1)}, bf16[256,6,128]{2,0,1:T(8,128)(2,1)}, u32[]{:S(2)}) copy-start(bf16[256,6,128]{2,0,1:T(8,128)(2,1)} %param.16) | copy-start | bytes 1179652
  1.6 0.7 %copy-start.2 = (s32[3,64]{1,0:T(4,128)S(1)}, s32[3,64]{1,0:T(4,128)}, u32[]{:S(2)}) copy-start(s32[3,64]{1,0:T(4,128)} %param.15) | copy-start | bytes 2308
  3.0 0.7 %copy-start.3 = (f32[128]{0:T(128)S(1)}, f32[128]{0:T(128)}, u32[]{:S(2)}) copy-start(f32[128]{0:T(128)} %constant.65) | copy-start | bytes 1540
  3.0 0.7 %copy-start.4 = (pred[128]{0:T(512)(128)(4,1)S(1)}, pred[128]{0:T(512)(128)(4,1)}, u32[]{:S(2)}) copy-start(pred[128]{0:T(512)(128)(4,1)} %constant.64) | copy-start | bytes 388
  3.0 0.7 %copy-start.5 = (pred[128]{0:T(512)(128)(4,1)S(1)}, pred[128]{0:T(512)(128)(4,1)}, u32[]{:S(2)}) copy-start(pred[128]{0:T(512)(128)(4,1)} %constant.63) | copy-start | bytes 388
  46.6 1.6 %copy-start.1 = (bf16[2,3,32,128]{3,2,1,0:T(8,128)(2,1)S(1)}, bf16[2,3,32,128]{3,2,1,0:T(8,128)(2,1)}, u32[]{:S(2)}) copy-start(bf16[2,3,32,128]{3,2,1,0:T(8,128)(2,1)} %get-tuple-element.5) | copy-start | bytes 147460

commit v2 on v1

--- a/solution.py
+++ b/solution.py
@@ -22,20 +22,18 @@
 
 
 def constants(dim):
-    axis = np.zeros((dim,), np.int32)
     freq = np.zeros((dim,), np.float32)
     swap = np.zeros((dim, dim), np.float32)
     start = 0
-    for index, size in enumerate(bands(dim)):
+    for size in bands(dim):
         half = size // 2
         for i in range(half):
             low, high = start + i, start + half + i
-            axis[low] = axis[high] = index
             freq[low] = freq[high] = np.float32(THETA ** (-2.0 * i / size))
             swap[high, low] = -1.0
             swap[low, high] = 1.0
         start += size
-    return axis, freq, swap
+    return freq, swap
 
 
 def each(count, body):
@@ -46,9 +44,9 @@
         lax.fori_loop(0, count, lambda i, _: (body(i), 0)[1], 0)
 
 
-def kernel(far, hds, q_ref, k_ref, v_ref, cos_ref, sin_ref, swap_ref, tq_ref, tk_ref, tv_ref, count_ref,
-           out_ref, tout_ref, qs, ks, qg, kv, ost, tst, acc, peak, total,
-           a_send, q_recv, kv_recv, f_send, n_send, o_send, o_recv, t_sems):
+def kernel(far, hds, q_ref, k_ref, v_ref, tq_ref, tk_ref, tv_ref, pos_ref, freq_ref, swap_ref, count_ref,
+           out_ref, tout_ref, qin, kin, tqs, tks, tvs, qs, ks, qg, kv, ost, tst, acc, peak, total, probs,
+           in_sems, a_send, q_recv, kv_recv, f_send, n_send, o_send, o_recv, t_sems):
     ctx = lax.axis_index("ctx")
     hd = lax.axis_index("hd")
     fi, mi, ni = ctx // (PAIR * NEAR), (ctx // NEAR) % PAIR, ctx % NEAR
@@ -73,6 +71,17 @@
         n = lax.rem(ni + d, NEAR)
         return n, at(fi, mi, n, hd)
 
+    text_heads = pl.ds(mi * heads, heads)
+    k_in = pltpu.make_async_copy(k_ref, kin, in_sems.at[0])
+    q_in = pltpu.make_async_copy(q_ref, qin, in_sems.at[1])
+    v_in = pltpu.make_async_copy(v_ref.at[mine], kv.at[slot, 1, mine], in_sems.at[2])
+    text_in = (
+        pltpu.make_async_copy(tq_ref.at[text_heads], tqs, in_sems.at[3]),
+        pltpu.make_async_copy(tk_ref.at[text_heads], tks, in_sems.at[4]),
+        pltpu.make_async_copy(tv_ref.at[text_heads], tvs, in_sems.at[5]),
+    )
+    for copy in (k_in, q_in, v_in) + text_in:
+        copy.start()
     barrier = pltpu.get_barrier_semaphore()
 
     def greet(peer):
@@ -82,7 +91,18 @@
     each(far - 1, lambda i: greet(far_peer(i + 1)[1]))
     each(NEAR - 1, lambda i: greet(near_peer(i + 1)[1]))
 
-    cos, sin, swap = cos_ref[...], sin_ref[...], swap_ref[...]
+    swap = swap_ref[...]
+    diagonal = (lax.broadcasted_iota(jnp.int32, (tokens, tokens), 0)
+                == lax.broadcasted_iota(jnp.int32, (tokens, tokens), 1))
+    lane = lax.broadcasted_iota(jnp.int32, (tokens, dim), 1)
+
+    def column(axis):
+        row = pos_ref[axis:axis + 1, :].astype(jnp.float32)
+        return jnp.sum(jnp.where(diagonal, row, 0.0), axis=1, keepdims=True)
+
+    band_t, band_h, _ = bands(dim)
+    angle = jnp.where(lane < band_t, column(0), jnp.where(lane < band_t + band_h, column(1), column(2))) * freq_ref[...]
+    cos, sin = jnp.cos(angle), jnp.sin(angle)
 
     def rotate(src, dst):
         for g in range(groups):
@@ -91,11 +111,13 @@
                 turned = jnp.dot(x, swap, preferred_element_type=jnp.float32)
                 dst[g, h] = (x.astype(jnp.float32) * cos + turned * sin).astype(jnp.bfloat16)
 
-    rotate(k_ref, ks)
-    rotate(q_ref, qs)
+    k_in.wait()
+    rotate(kin, ks)
+    q_in.wait()
+    rotate(qin, qs)
     kv[slot, 0, mine] = ks[mine]
-    kv[slot, 1, mine] = v_ref[mine]
     qg[mine] = qs[mine]
+    v_in.wait()
     pl.semaphore_wait(barrier, (groups - 1) + (far - 1) + (NEAR - 1))
 
     def remote(src, dst, send, recv, peer):
@@ -133,9 +155,8 @@
         for d in range(1, groups):
             kv_to_group(w, d).start()
         spread(w, mine)
-        if w == 0:
-            for d in range(1, groups):
-                q_to_group(d).start()
+    for d in range(1, groups):
+        q_to_group(d).start()
     for w in range(2):
         for d in range(1, groups):
             g = lax.rem(mine + d, groups)
@@ -146,7 +167,8 @@
     rows = groups * tokens
 
     def queries(h):
-        return jnp.concatenate([qg[:, h].reshape(rows, dim), tq_ref[h]], axis=0)
+        own_text = [tqs[h, (fi * PAIR + m) * NEAR + ni] for m in range(PAIR)]
+        return jnp.concatenate([qg[:, h].reshape(rows, dim)] + own_text, axis=0)
 
     def score(h, keys):
         return lax.dot_general(queries(h), keys, (((1,), (1,)), ((), ())), preferred_element_type=jnp.float32) * scale
@@ -154,20 +176,27 @@
     for d in range(1, groups):
         g = lax.rem(mine + d, groups)
         remote(qg.at[g], qg.at[g], a_send.at[2, d], q_recv.at[g], group_peer(d)[1]).wait_recv()
-
-    for h in range(heads):
-        s = score(h, tk_ref[h])
-        live = lax.broadcasted_iota(jnp.int32, s.shape, 1) < count_ref[0]
-        s = jnp.where(live, s, -jnp.inf)
-        top = jnp.max(s, axis=1, keepdims=True)
-        p = jnp.exp2(s - top)
-        peak[h] = top
-        total[h] = jnp.sum(p, axis=1, keepdims=True)
-        acc[h] = jnp.dot(p.astype(jnp.bfloat16), tv_ref[h], preferred_element_type=jnp.float32)
-
-    def absorb(h, s):
-        keys = kv[s, 0, :, h].reshape(rows, dim)
-        values = kv[s, 1, :, h].reshape(rows, dim)
+    for copy in text_in:
+        copy.wait()
+
+    def start_text():
+        for h in range(heads):
+            s = score(h, tks[h])
+            live = lax.broadcasted_iota(jnp.int32, s.shape, 1) < count_ref[0]
+            s = jnp.where(live, s, -jnp.inf)
+            top = jnp.max(s, axis=1, keepdims=True)
+            p = jnp.exp2(s - top)
+            peak[h] = top
+            total[h] = jnp.sum(p, axis=1, keepdims=True)
+            acc[h] = jnp.dot(p.astype(jnp.bfloat16), tvs[h], preferred_element_type=jnp.float32)
+
+    def keys_of(s, h):
+        return kv[s, 0, :, h].reshape(rows, dim)
+
+    def values_of(s, h):
+        return kv[s, 1, :, h].reshape(rows, dim)
+
+    def weigh(h, keys):
         sc = score(h, keys)
         old = peak[h]
         top = jnp.maximum(old, jnp.max(sc, axis=1, keepdims=True))
@@ -175,45 +204,62 @@
         factor = jnp.exp2(old - top)
         peak[h] = top
         total[h] = total[h] * factor + jnp.sum(p, axis=1, keepdims=True)
-        acc[h] = acc[h] * factor + jnp.dot(p.astype(jnp.bfloat16), values, preferred_element_type=jnp.float32)
-
-    for h in range(heads):
-        absorb(h, slot)
-
-    def relay(i):
-        s = far_peer(i + 1)[0] * NEAR + ni
+        return p.astype(jnp.bfloat16), factor
+
+    def absorb(s):
+        for h in range(heads):
+            p, factor = weigh(h, keys_of(s, h))
+            acc[h] = acc[h] * factor + jnp.dot(p, values_of(s, h), preferred_element_type=jnp.float32)
+
+    other = near_peer(1)[0]
+    near_slot = fi * NEAR + other
+
+    def from_far(i):
+        f = far_peer(i + 1)[0]
+        return f * NEAR + ni, f * NEAR + other
+
+    def relay(i, w, d):
+        s, g = from_far(i)[0], lax.rem(mine + d, groups)
+        arrived(s, w, g)
+        kv_to_near(s, w, g, 1).start()
+
+    def take(s, w):
+        for d in range(groups):
+            arrived(s, w, lax.rem(mine + d, groups))
+
+    def whole(i):
         for w in range(2):
             for d in range(groups):
-                g = lax.rem(mine + d, groups)
-                arrived(s, w, g)
-                kv_to_near(s, w, g, 1).start()
-    each(far - 1, relay)
-
-    other = near_peer(1)[0]
-
-    def take(s):
-        for w in range(2):
-            for d in range(groups):
-                arrived(s, w, lax.rem(mine + d, groups))
-
-    near_slot = fi * NEAR + other
-    take(near_slot)
+                relay(i, w, d)
+        straight, across = from_far(i)
+        absorb(straight)
+        take(across, 0)
+        take(across, 1)
+        absorb(across)
+
+    start_text()
+    each(far - 2, whole)
+    last = far - 2
+    straight, across = from_far(last)
+    relay(last, 0, 0)
+    relay(last, 1, 0)
+    absorb(slot)
+    for d in range(1, groups):
+        relay(last, 0, d)
+    take(near_slot, 0)
+    take(near_slot, 1)
+    absorb(near_slot)
+    relay(last, 1, 1)
+    take(across, 0)
     for h in range(heads):
-        absorb(h, near_slot)
-
-    def from_far(i):
-        for h in range(heads):
-            absorb(h, far_peer(i + 1)[0] * NEAR + ni)
-    each(far - 1, from_far)
-
-    def across(i):
-        s = far_peer(i + 1)[0] * NEAR + other
-        take(s)
-        for h in range(heads):
-            absorb(h, s)
-    each(far - 2, across)
-    last = far_peer(far - 1)[0] * NEAR + other
-    take(last)
+        p, factor = weigh(h, jnp.concatenate([keys_of(straight, h), keys_of(across, h)], axis=0))
+        probs[h] = p
+        acc[h] = acc[h] * factor
+    for d in range(2, groups):
+        relay(last, 1, d)
+    for h in range(heads):
+        acc[h] += jnp.dot(probs[h, :, :rows], values_of(straight, h), preferred_element_type=jnp.float32)
+    take(across, 1)
 
     def out_to(h, d):
         g, peer = group_peer(d)
@@ -226,8 +272,8 @@
                       at(fi, partner, ni, hd))
 
     for h in range(heads):
-        absorb(h, last)
-        result = (acc[h] / total[h]).astype(jnp.bfloat16)
+        mixed = acc[h] + jnp.dot(probs[h, :, rows:], values_of(across, h), preferred_element_type=jnp.float32)
+        result = (mixed / total[h]).astype(jnp.bfloat16)
         ost[h] = result[:rows].reshape(groups, tokens, dim)
         tst[h] = result[rows:].reshape(tst.shape[1:])
         for d in range(1, groups):
@@ -263,24 +309,11 @@
     far = ctxs // (PAIR * NEAR)
     share = text // ctxs
     rows = groups * tokens + PAIR * share
-    axis, freq, swap = constants(dim)
-    pos = positions.astype(jnp.float32)[:, :, None]
-    lane_axis = axis[None, :]
-    angle = jnp.where(lane_axis == 0, pos[0], jnp.where(lane_axis == 1, pos[1], pos[2])) * freq[None, :]
-    cos, sin = jnp.cos(angle), jnp.sin(angle)
+    freq, swap = constants(dim)
 
     def by_head(x):
         return jnp.swapaxes(x, 0, 1).reshape(groups, heads, tokens, dim)
 
-    ctx = lax.axis_index("ctx")
-    fi, mi, ni = ctx // (PAIR * NEAR), (ctx // NEAR) % PAIR, ctx % NEAR
-
-    def text_heads(x):
-        return jnp.swapaxes(lax.dynamic_slice_in_dim(x, mi * heads, heads, 1), 0, 1)
-
-    tq = text_q.reshape(far, PAIR, NEAR, share, PAIR * heads, dim)
-    tq = lax.dynamic_slice(tq, (fi, 0, ni, 0, mi * heads, 0), (1, PAIR, 1, share, heads, dim))
-    tq = jnp.swapaxes(tq.reshape(PAIR * share, heads, dim), 0, 1)
     vmem = pl.BlockSpec(memory_space=pltpu.VMEM)
     dma = pltpu.SemaphoreType.DMA
     slots = far * NEAR
@@ -291,9 +324,14 @@
             jax.ShapeDtypeStruct((groups, heads, tokens, dim), jnp.bfloat16),
             jax.ShapeDtypeStruct((PAIR, heads, share, dim), jnp.bfloat16),
         ),
-        in_specs=[vmem] * 9 + [pl.BlockSpec(memory_space=pltpu.SMEM)],
+        in_specs=[pl.BlockSpec(memory_space=pl.ANY)] * 6 + [vmem] * 3 + [pl.BlockSpec(memory_space=pltpu.SMEM)],
         out_specs=(vmem, vmem),
         scratch_shapes=[
+            pltpu.VMEM((groups, heads, tokens, dim), jnp.bfloat16),
+            pltpu.VMEM((groups, heads, tokens, dim), jnp.bfloat16),
+            pltpu.VMEM((heads, ctxs, share, dim), jnp.bfloat16),
+            pltpu.VMEM((heads, text, dim), jnp.bfloat16),
+            pltpu.VMEM((heads, text, dim), jnp.bfloat16),
             pltpu.VMEM((groups, heads, tokens, dim), jnp.bfloat16),
             pltpu.VMEM((groups, heads, tokens, dim), jnp.bfloat16),
             pltpu.VMEM((groups, heads, tokens, dim), jnp.bfloat16),
@@ -303,6 +341,8 @@
             pltpu.VMEM((heads, rows, dim), jnp.float32),
             pltpu.VMEM((heads, rows, 1), jnp.float32),
             pltpu.VMEM((heads, rows, 1), jnp.float32),
+            pltpu.VMEM((heads, rows, 2 * groups * tokens), jnp.bfloat16),
+            dma((6,)),
             dma((3, groups)),
             dma((groups,)),
             dma((slots, 2, groups)),
@@ -316,8 +356,9 @@
             collective_id=0, has_side_effects=True, vmem_limit_bytes=60 * 1024 * 1024
         ),
     )(
-        by_head(video_q), by_head(video_k), by_head(video_v), cos, sin, jnp.asarray(swap, jnp.bfloat16),
-        tq, text_heads(text_k), text_heads(text_v), text_count,
+        by_head(video_q), by_head(video_k), by_head(video_v),
+        jnp.swapaxes(text_q, 0, 1).reshape(PAIR * heads, ctxs, share, dim), jnp.swapaxes(text_k, 0, 1), jnp.swapaxes(text_v, 0, 1),
+        positions, jnp.asarray(freq[None, :]), jnp.asarray(swap, jnp.bfloat16), text_count,
     )
     video_out = jnp.swapaxes(out.reshape(all_heads, tokens, dim), 0, 1)
     text_out = jnp.swapaxes(tout.reshape(PAIR * heads, share, dim), 0, 1)

time: 49.1 us -> 43.3 us (0.88)
  local copies, waits for them, and re-layouts: 6.3 us -> 2.25 us
  other arithmetic: 0.85 us -> 0 us
  Pallas kernels: 40.3 us -> 39.5 us
    transpose x1 -> x0, local copies, waits for them, and re-layouts: 1.78 us -> none  [text_heads(): return jnp.swapaxes(lax.dynamic_slice_in_dim(x, mi * heads, heads, 1), 0, 1)]
    unnamed x14 -> x4, local copies, waits for them, and re-layouts: 3.89 us -> 2.25 us
    sin x1 -> x0, other arithmetic: 0.85 us -> none  [local(): cos, sin = (jnp.cos(angle), jnp.sin(angle))]
    pallas_call x1, Pallas kernels: 40.3 us -> 39.5 us  [local(): pl.pallas_call(functools.partial(kernel, far, hds), name='joint_attention...]
    dynamic_slice x1 -> x0, local copies, waits for them, and re-layouts: 0.62 us -> none  [local(): lax.dynamic_slice(tq, (fi, 0, ni, 0, mi * heads, 0), (1, PAIR, 1, share,...]
where the time goes in v2:
time: 43.3 us; the launch traced here: 43.1 us
  Pallas kernels  39.5 us (91%)
  local copies, waits for them, and re-layouts  2.25 us (5%)
  between operations  1.3 us (3%)
    pallas_call x1, Pallas kernels, local(): pl.pallas_call(functools.partial(kernel, far, hds), name='joint_attention...  39.5 us
    unnamed x4, local copies, waits for them, and re-layouts  2.25 us

profile of v2, /device:TPU:0, one launch (start us, length us, event | category | flops | bytes accessed | tf_op | source)
XLA Modules:
  0.0 43.1 jit_solution(10590551758677862549)
XLA Ops:
  1.3 39.5 %joint_attention.1 = (bf16[4,3,64,128]{3,2,1,0:T(8,128)(2,1)}, bf16[2,3,32,128]{3,2,1,0:T(8,128)(2,1)}) custom-call(bf16[4,3,64,128]{3,2,1,0:T(8,128)(2,1)} %bitcast.24, bf16[4,3,64,128]{3,2,1,0:T(8,128)(2,1)} %bitcast.25, bf16[4,3,64,128]{3,2,1,0:T(8,128)(2,1)} %bitcast.26, bf16[6,8,32,128]{3,2,1,0:T(8,128)(2,1)} %bitcast.20, ...), custom_call_target="tpu_custom_call" | custom-call | tf_op jit(solution)/shard_map/joint_attention/pallas_call | solution.py:320
  40.8 0.0 copy-start
  40.8 1.6 %copy.15 = bf16[64,12,128]{2,0,1:T(8,128)(2,1)} copy(bf16[64,12,128]{2,0,1:T(8,128)(2,1)} %bitcast.23) | data formatting | bytes 393216
  42.4 0.0 copy-done
  42.4 0.6 %copy.16 = bf16[32,6,128]{2,0,1:T(8,128)(2,1)} copy(bf16[32,6,128]{2,0,1:T(8,128)(2,1)S(1)} %bitcast.27) | data formatting | bytes 98304
Async XLA Ops:
  40.8 1.6 %copy-start = (bf16[2,3,32,128]{3,2,1,0:T(8,128)(2,1)S(1)}, bf16[2,3,32,128]{3,2,1,0:T(8,128)(2,1)}, u32[]{:S(2)}) copy-start(bf16[2,3,32,128]{3,2,1,0:T(8,128)(2,1)} %get-tuple-element.5) | copy-start | bytes 147460

commit v3 on v2

--- a/solution.py
+++ b/solution.py
@@ -154,9 +154,10 @@
     for w in range(2):
         for d in range(1, groups):
             kv_to_group(w, d).start()
-        spread(w, mine)
     for d in range(1, groups):
         q_to_group(d).start()
+    for w in range(2):
+        spread(w, mine)
     for w in range(2):
         for d in range(1, groups):
             g = lax.rem(mine + d, groups)
@@ -299,6 +300,11 @@
         text_to(h).wait_send()
         remote(tst.at[h, partner], tout_ref.at[partner, h], t_sems.at[0, h], t_sems.at[1, h],
                at(fi, partner, ni, hd)).wait_recv()
+
+
+def settle(out_ref, tout_ref, video_ref, text_ref):
+    video_ref[...] = out_ref[...]
+    text_ref[...] = tout_ref[...]
 
 
 def local(ctxs, hds, video_q, video_k, video_v, positions, text_q, text_k, text_v, text_count):
@@ -360,6 +366,13 @@
         jnp.swapaxes(text_q, 0, 1).reshape(PAIR * heads, ctxs, share, dim), jnp.swapaxes(text_k, 0, 1), jnp.swapaxes(text_v, 0, 1),
         positions, jnp.asarray(freq[None, :]), jnp.asarray(swap, jnp.bfloat16), text_count,
     )
+    out, tout = pl.pallas_call(
+        settle,
+        name="settle",
+        out_shape=(jax.ShapeDtypeStruct(out.shape, out.dtype), jax.ShapeDtypeStruct(tout.shape, tout.dtype)),
+        in_specs=[vmem] * 2,
+        out_specs=(vmem, vmem),
+    )(out, tout)
     video_out = jnp.swapaxes(out.reshape(all_heads, tokens, dim), 0, 1)
     text_out = jnp.swapaxes(tout.reshape(PAIR * heads, share, dim), 0, 1)
     return (video_out, text_out)

time: 43.3 us -> 41.9 us (0.968)
  local copies, waits for them, and re-layouts: 2.25 us -> 0 us
  Pallas kernels: 39.5 us -> 40.3 us
    unnamed x4 -> x0, local copies, waits for them, and re-layouts: 2.25 us -> none
    pallas_call x0 -> x1, Pallas kernels: none -> 1.63 us  [local(): pl.pallas_call(settle, name='settle', out_shape=(jax.ShapeDtypeStruct(out...]
    pallas_call x1, Pallas kernels: 39.5 us -> 38.7 us  [local(): pl.pallas_call(functools.partial(kernel, far, hds), name='joint_attention...]
where the time goes in v3:
time: 41.9 us; the launch traced here: 41.6 us
  Pallas kernels  40.3 us (96%)
  between operations  1.29 us (3%)
    pallas_call x1, Pallas kernels, local(): pl.pallas_call(functools.partial(kernel, far, hds), name='joint_attention...  38.7 us
    pallas_call x1, Pallas kernels, local(): pl.pallas_call(settle, name='settle', out_shape=(jax.ShapeDtypeStruct(out...  1.63 us

profile of v3, /device:TPU:0, one launch (start us, length us, event | category | flops | bytes accessed | tf_op | source)
XLA Modules:
  0.0 41.6 jit_solution(8754705441231490155)
XLA Ops:
  1.3 38.7 %joint_attention.1 = (bf16[4,3,64,128]{3,2,1,0:T(8,128)(2,1)}, bf16[2,3,32,128]{3,2,1,0:T(8,128)(2,1)}) custom-call(bf16[4,3,64,128]{3,2,1,0:T(8,128)(2,1)} %bitcast.23, bf16[4,3,64,128]{3,2,1,0:T(8,128)(2,1)} %bitcast.24, bf16[4,3,64,128]{3,2,1,0:T(8,128)(2,1)} %bitcast.25, bf16[6,8,32,128]{3,2,1,0:T(8,128)(2,1)} %bitcast.20, ...), custom_call_target="tpu_custom_call" | custom-call | tf_op jit(solution)/shard_map/joint_attention/pallas_call | solution.py:326
  40.0 1.6 %settle.1 = (bf16[4,3,64,128]{3,2,1,0:T(8,128)(2,1)}, bf16[2,3,32,128]{3,2,1,0:T(8,128)(2,1)}) custom-call(bf16[4,3,64,128]{3,2,1,0:T(8,128)(2,1)} %get-tuple-element.6.out_ref, bf16[2,3,32,128]{3,2,1,0:T(8,128)(2,1)} %get-tuple-element.7.tout_ref), custom_call_target="tpu_custom_call" | custom-call | tf_op jit(solution)/shard_map/settle/pallas_call | solution.py:369

commit v4 on v3

--- a/solution.py
+++ b/solution.py
@@ -44,8 +44,8 @@
         lax.fori_loop(0, count, lambda i, _: (body(i), 0)[1], 0)
 
 
-def kernel(far, hds, q_ref, k_ref, v_ref, tq_ref, tk_ref, tv_ref, pos_ref, freq_ref, swap_ref, count_ref,
-           out_ref, tout_ref, qin, kin, tqs, tks, tvs, qs, ks, qg, kv, ost, tst, acc, peak, total, probs,
+def kernel(far, hds, q_ref, k_ref, v_ref, tq_ref, tk_ref, tv_ref, pos_in, freq_in, swap_in, count_ref,
+           out_ref, tout_ref, pos_ref, freq_ref, swap_ref, qin, kin, tqs, tks, tvs, qs, ks, qg, kv, ost, tst, acc, peak, total, probs,
            in_sems, a_send, q_recv, kv_recv, f_send, n_send, o_send, o_recv, t_sems):
     ctx = lax.axis_index("ctx")
     hd = lax.axis_index("hd")
@@ -59,9 +59,17 @@
     def at(f, m, n, h):
         return {"ctx": (f * PAIR + m) * NEAR + n, "hd": h}
 
+    def group_of(d):
+        return lax.rem(hd + d // PAIR, hds) * PAIR + lax.rem(mi + d % PAIR, PAIR)
+
     def group_peer(d):
-        g = lax.rem(mine + d, groups)
+        g = group_of(d)
         return g, at(fi, g % PAIR, ni, g // PAIR)
+
+    straight_first = [d for d in range(PAIR, groups, PAIR)]
+    rest = [d for d in range(1, groups) if d % PAIR]
+    early = [(0, 0), (1, 0)] + [(w, d) for d in straight_first for w in range(2)] + [(0, d) for d in rest]
+    late = [(1, d) for d in rest]
 
     def far_peer(d):
         f = lax.rem(fi + d, far)
@@ -80,8 +88,11 @@
         pltpu.make_async_copy(tk_ref.at[text_heads], tks, in_sems.at[4]),
         pltpu.make_async_copy(tv_ref.at[text_heads], tvs, in_sems.at[5]),
     )
-    for copy in (k_in, q_in, v_in) + text_in:
-        copy.start()
+    table_in = (
+        pltpu.make_async_copy(pos_in, pos_ref, in_sems.at[6]),
+        pltpu.make_async_copy(freq_in, freq_ref, in_sems.at[7]),
+        pltpu.make_async_copy(swap_in, swap_ref, in_sems.at[8]),
+    )
     barrier = pltpu.get_barrier_semaphore()
 
     def greet(peer):
@@ -91,6 +102,10 @@
     each(far - 1, lambda i: greet(far_peer(i + 1)[1]))
     each(NEAR - 1, lambda i: greet(near_peer(i + 1)[1]))
 
+    for copy in table_in + (k_in, q_in, v_in) + text_in:
+        copy.start()
+    for copy in table_in:
+        copy.wait()
     swap = swap_ref[...]
     diagonal = (lax.broadcasted_iota(jnp.int32, (tokens, tokens), 0)
                 == lax.broadcasted_iota(jnp.int32, (tokens, tokens), 1))
@@ -151,18 +166,16 @@
         each(far - 1, lambda i: kv_to_far(w, g, i + 1).start())
         kv_to_near(slot, w, g, 1).start()
 
-    for w in range(2):
-        for d in range(1, groups):
-            kv_to_group(w, d).start()
-    for d in range(1, groups):
+    for w, d in (early + late)[2:]:
+        kv_to_group(w, d).start()
+    for d in straight_first + rest:
         q_to_group(d).start()
     for w in range(2):
         spread(w, mine)
-    for w in range(2):
-        for d in range(1, groups):
-            g = lax.rem(mine + d, groups)
-            arrived(slot, w, g)
-            spread(w, g)
+    for w, d in (early + late)[2:]:
+        g = group_of(d)
+        arrived(slot, w, g)
+        spread(w, g)
 
     scale = math.log2(math.e) / math.sqrt(dim)
     rows = groups * tokens
@@ -175,7 +188,7 @@
         return lax.dot_general(queries(h), keys, (((1,), (1,)), ((), ())), preferred_element_type=jnp.float32) * scale
 
     for d in range(1, groups):
-        g = lax.rem(mine + d, groups)
+        g = group_of(d)
         remote(qg.at[g], qg.at[g], a_send.at[2, d], q_recv.at[g], group_peer(d)[1]).wait_recv()
     for copy in text_in:
         copy.wait()
@@ -220,18 +233,17 @@
         return f * NEAR + ni, f * NEAR + other
 
     def relay(i, w, d):
-        s, g = from_far(i)[0], lax.rem(mine + d, groups)
+        s, g = from_far(i)[0], group_of(d)
         arrived(s, w, g)
         kv_to_near(s, w, g, 1).start()
 
     def take(s, w):
         for d in range(groups):
-            arrived(s, w, lax.rem(mine + d, groups))
+            arrived(s, w, group_of(d))
 
     def whole(i):
-        for w in range(2):
-            for d in range(groups):
-                relay(i, w, d)
+        for w, d in early + late:
+            relay(i, w, d)
         straight, across = from_far(i)
         absorb(straight)
         take(across, 0)
@@ -245,19 +257,18 @@
     relay(last, 0, 0)
     relay(last, 1, 0)
     absorb(slot)
-    for d in range(1, groups):
-        relay(last, 0, d)
+    for w, d in early[2:]:
+        relay(last, w, d)
     take(near_slot, 0)
     take(near_slot, 1)
     absorb(near_slot)
-    relay(last, 1, 1)
     take(across, 0)
     for h in range(heads):
         p, factor = weigh(h, jnp.concatenate([keys_of(straight, h), keys_of(across, h)], axis=0))
         probs[h] = p
         acc[h] = acc[h] * factor
-    for d in range(2, groups):
-        relay(last, 1, d)
+    for w, d in late:
+        relay(last, w, d)
     for h in range(heads):
         acc[h] += jnp.dot(probs[h, :, :rows], values_of(straight, h), preferred_element_type=jnp.float32)
     take(across, 1)
@@ -289,7 +300,7 @@
         q_to_group(d).wait_send()
     for w in range(2):
         for d in range(groups):
-            g = lax.rem(mine + d, groups)
+            g = group_of(d)
             each(far - 1, lambda i: kv_to_far(w, g, i + 1).wait_send())
             each(far, lambda i: kv_to_near(far_peer(i)[0] * NEAR + ni, w, g, 1).wait_send())
     for h in range(heads):
@@ -323,6 +334,7 @@
     vmem = pl.BlockSpec(memory_space=pltpu.VMEM)
     dma = pltpu.SemaphoreType.DMA
     slots = far * NEAR
+    room = 12 * 2**20 + slots * 2 * all_heads * tokens * dim * 3
     out, tout = pl.pallas_call(
         functools.partial(kernel, far, hds),
         name="joint_attention",
@@ -330,9 +342,12 @@
             jax.ShapeDtypeStruct((groups, heads, tokens, dim), jnp.bfloat16),
             jax.ShapeDtypeStruct((PAIR, heads, share, dim), jnp.bfloat16),
         ),
-        in_specs=[pl.BlockSpec(memory_space=pl.ANY)] * 6 + [vmem] * 3 + [pl.BlockSpec(memory_space=pltpu.SMEM)],
+        in_specs=[pl.BlockSpec(memory_space=pltpu.HBM)] * 9 + [pl.BlockSpec(memory_space=pltpu.SMEM)],
         out_specs=(vmem, vmem),
         scratch_shapes=[
+            pltpu.VMEM(positions.shape, jnp.int32),
+            pltpu.VMEM((1, dim), jnp.float32),
+            pltpu.VMEM((dim, dim), jnp.bfloat16),
             pltpu.VMEM((groups, heads, tokens, dim), jnp.bfloat16),
             pltpu.VMEM((groups, heads, tokens, dim), jnp.bfloat16),
             pltpu.VMEM((heads, ctxs, share, dim), jnp.bfloat16),
@@ -348,7 +363,7 @@
             pltpu.VMEM((heads, rows, 1), jnp.float32),
             pltpu.VMEM((heads, rows, 1), jnp.float32),
             pltpu.VMEM((heads, rows, 2 * groups * tokens), jnp.bfloat16),
-            dma((6,)),
+            dma((9,)),
             dma((3, groups)),
             dma((groups,)),
             dma((slots, 2, groups)),
@@ -359,7 +374,7 @@
             dma((2, heads)),
         ],
         compiler_params=pltpu.CompilerParams(
-            collective_id=0, has_side_effects=True, vmem_limit_bytes=60 * 1024 * 1024
+            collective_id=0, has_side_effects=True, vmem_limit_bytes=room
         ),
     )(
         by_head(video_q), by_head(video_k), by_head(video_v),
@@ -372,6 +387,7 @@
         out_shape=(jax.ShapeDtypeStruct(out.shape, out.dtype), jax.ShapeDtypeStruct(tout.shape, tout.dtype)),
         in_specs=[vmem] * 2,
         out_specs=(vmem, vmem),
+        compiler_params=pltpu.CompilerParams(vmem_limit_bytes=4 * 2**20),
     )(out, tout)
     video_out = jnp.swapaxes(out.reshape(all_heads, tokens, dim), 0, 1)
     text_out = jnp.swapaxes(tout.reshape(PAIR * heads, share, dim), 0, 1)

time: 41.9 us -> 47.6 us (1.14)
  local copies, waits for them, and re-layouts: 0 us -> 7.19 us
  Pallas kernels: 40.3 us -> 38.7 us
    unnamed x0 -> x18, local copies, waits for them, and re-layouts: none -> 7.19 us
    pallas_call x1, Pallas kernels: 1.63 us -> 0.7 us  [local(): pl.pallas_call(settle, name='settle', out_shape=(jax.ShapeDtypeStruct(out...]
    pallas_call x1, Pallas kernels: 38.7 us -> 38 us  [local(): pl.pallas_call(functools.partial(kernel, far, hds), name='joint_attention...]
where the time goes in v4:
time: 47.6 us; the launch traced here: 47.2 us
  Pallas kernels  38.7 us (81%)
  local copies, waits for them, and re-layouts  7.19 us (15%)
  between operations  1.31 us (3%)
    pallas_call x1, Pallas kernels, local(): pl.pallas_call(functools.partial(kernel, far, hds), name='joint_attention...  38 us
    unnamed x18, local copies, waits for them, and re-layouts  7.19 us

profile of v4, /device:TPU:0, one launch (start us, length us, event | category | flops | bytes accessed | tf_op | source)
XLA Modules:
  0.0 47.2 jit_solution(10075950619470006918)
XLA Ops:
  1.3 0.0 copy-start.7
  1.3 0.0 copy-start.8
  1.3 0.7 %copy-done.7 = s32[3,64]{1,0:T(4,128)S(1)} copy-done((s32[3,64]{1,0:T(4,128)S(1)}, s32[3,64]{1,0:T(4,128)}, u32[]{:S(2)}) %copy-start.7) | copy-done | bytes 792
  2.0 0.0 copy-done.8
  2.0 0.0 copy-start
  2.0 1.0 %copy-done = bf16[256,6,128]{2,0,1:T(8,128)(2,1)S(1)} copy-done((bf16[256,6,128]{2,0,1:T(8,128)(2,1)S(1)}, bf16[256,6,128]{2,0,1:T(8,128)(2,1)}, u32[]{:S(2)}) %copy-start) | copy-done | bytes 393240
  3.0 0.0 copy-start.1
  3.0 1.0 %copy-done.1 = bf16[256,6,128]{2,0,1:T(8,128)(2,1)S(1)} copy-done((bf16[256,6,128]{2,0,1:T(8,128)(2,1)S(1)}, bf16[256,6,128]{2,0,1:T(8,128)(2,1)}, u32[]{:S(2)}) %copy-start.1) | copy-done | bytes 393240
  4.0 0.0 copy-start.2
  4.0 1.0 %copy-done.2 = bf16[256,6,128]{2,0,1:T(8,128)(2,1)S(1)} copy-done((bf16[256,6,128]{2,0,1:T(8,128)(2,1)S(1)}, bf16[256,6,128]{2,0,1:T(8,128)(2,1)}, u32[]{:S(2)}) %copy-start.2) | copy-done | bytes 393240
  5.0 0.0 copy-start.3
  5.0 0.9 %copy-done.3 = bf16[64,12,128]{2,0,1:T(8,128)(2,1)S(1)} copy-done((bf16[64,12,128]{2,0,1:T(8,128)(2,1)S(1)}, bf16[64,12,128]{2,0,1:T(8,128)(2,1)}, u32[]{:S(2)}) %copy-start.3) | copy-done | bytes 196632
  5.9 0.0 copy-start.4
  5.9 0.9 %copy-done.4 = bf16[64,12,128]{2,0,1:T(8,128)(2,1)S(1)} copy-done((bf16[64,12,128]{2,0,1:T(8,128)(2,1)S(1)}, bf16[64,12,128]{2,0,1:T(8,128)(2,1)}, u32[]{:S(2)}) %copy-start.4) | copy-done | bytes 196632
  6.8 0.0 copy-start.5
  6.8 0.9 %copy-done.5 = bf16[64,12,128]{2,0,1:T(8,128)(2,1)S(1)} copy-done((bf16[64,12,128]{2,0,1:T(8,128)(2,1)S(1)}, bf16[64,12,128]{2,0,1:T(8,128)(2,1)}, u32[]{:S(2)}) %copy-start.5) | copy-done | bytes 196632
  7.7 0.0 copy-start.6
  7.7 0.8 %copy-done.6 = bf16[128,128]{1,0:T(8,128)(2,1)S(1)} copy-done((bf16[128,128]{1,0:T(8,128)(2,1)S(1)}, bf16[128,128]{1,0:T(8,128)(2,1)}, u32[]{:S(2)}) %copy-start.6) | copy-done | bytes 32792
  8.5 38.0 %joint_attention.1 = (bf16[4,3,64,128]{3,2,1,0:T(8,128)(2,1)S(1)}, bf16[2,3,32,128]{3,2,1,0:T(8,128)(2,1)S(1)}) custom-call(bf16[4,3,64,128]{3,2,1,0:T(8,128)(2,1)S(1)} %bitcast.23, bf16[4,3,64,128]{3,2,1,0:T(8,128)(2,1)S(1)} %bitcast.24, bf16[4,3,64,128]{3,2,1,0:T(8,128)(2,1)S(1)} %bitcast.25, bf16[6,8,32,128]{3,2,1,0:T(8,128)(2,1)S(1)} %bitcast.20, ...), custom_call_target="tpu_custom_call" | custom-call | tf_op jit(solution)/shard_map/joint_attention/pallas_call | solution.py:338
  46.5 0.7 %settle.1 = (bf16[4,3,64,128]{3,2,1,0:T(8,128)(2,1)}, bf16[2,3,32,128]{3,2,1,0:T(8,128)(2,1)}) custom-call(bf16[4,3,64,128]{3,2,1,0:T(8,128)(2,1)S(1)} %get-tuple-element.6.out_ref, bf16[2,3,32,128]{3,2,1,0:T(8,128)(2,1)S(1)} %get-tuple-element.7.tout_ref), custom_call_target="tpu_custom_call" | custom-call | tf_op jit(solution)/shard_map/settle/pallas_call | solution.py:384
Async XLA Ops:
  1.3 0.7 %copy-start.7 = (s32[3,64]{1,0:T(4,128)S(1)}, s32[3,64]{1,0:T(4,128)}, u32[]{:S(2)}) copy-start(s32[3,64]{1,0:T(4,128)} %pos_in.1) | copy-start | bytes 2308
  1.3 0.7 %copy-start.8 = (f32[1,128]{1,0:T(1,128)S(1)}, f32[1,128]{1,0:T(1,128)}, u32[]{:S(2)}) copy-start(f32[1,128]{1,0:T(1,128)} %constant.4.clone.freq_in) | copy-start | bytes 1540
  2.0 1.0 %copy-start = (bf16[256,6,128]{2,0,1:T(8,128)(2,1)S(1)}, bf16[256,6,128]{2,0,1:T(8,128)(2,1)}, u32[]{:S(2)}) copy-start(bf16[256,6,128]{2,0,1:T(8,128)(2,1)} %param.14) | copy-start | bytes 1179652
  3.0 1.0 %copy-start.1 = (bf16[256,6,128]{2,0,1:T(8,128)(2,1)S(1)}, bf16[256,6,128]{2,0,1:T(8,128)(2,1)}, u32[]{:S(2)}) copy-start(bf16[256,6,128]{2,0,1:T(8,128)(2,1)} %param.15) | copy-start | bytes 1179652
  4.0 1.0 %copy-start.2 = (bf16[256,6,128]{2,0,1:T(8,128)(2,1)S(1)}, bf16[256,6,128]{2,0,1:T(8,128)(2,1)}, u32[]{:S(2)}) copy-start(bf16[256,6,128]{2,0,1:T(8,128)(2,1)} %param.16) | copy-start | bytes 1179652
  5.0 0.9 %copy-start.3 = (bf16[64,12,128]{2,0,1:T(8,128)(2,1)S(1)}, bf16[64,12,128]{2,0,1:T(8,128)(2,1)}, u32[]{:S(2)}) copy-start(bf16[64,12,128]{2,0,1:T(8,128)(2,1)} %param.10) | copy-start | bytes 589828
  5.9 0.9 %copy-start.4 = (bf16[64,12,128]{2,0,1:T(8,128)(2,1)S(1)}, bf16[64,12,128]{2,0,1:T(8,128)(2,1)}, u32[]{:S(2)}) copy-start(bf16[64,12,128]{2,0,1:T(8,128)(2,1)} %param.11) | copy-start | bytes 589828
  6.8 0.9 %copy-start.5 = (bf16[64,12,128]{2,0,1:T(8,128)(2,1)S(1)}, bf16[64,12,128]{2,0,1:T(8,128)(2,1)}, u32[]{:S(2)}) copy-start(bf16[64,12,128]{2,0,1:T(8,128)(2,1)} %param.12) | copy-start | bytes 589828
  7.7 0.8 %copy-start.6 = (bf16[128,128]{1,0:T(8,128)(2,1)S(1)}, bf16[128,128]{1,0:T(8,128)(2,1)}, u32[]{:S(2)}) copy-start(bf16[128,128]{1,0:T(8,128)(2,1)} %constant.5.clone.swap_in) | copy-start | bytes 98308

commit v5 on v4

--- a/solution.py
+++ b/solution.py
@@ -168,10 +168,10 @@
 
     for w, d in (early + late)[2:]:
         kv_to_group(w, d).start()
+    for w in range(2):
+        spread(w, mine)
     for d in straight_first + rest:
         q_to_group(d).start()
-    for w in range(2):
-        spread(w, mine)
     for w, d in (early + late)[2:]:
         g = group_of(d)
         arrived(slot, w, g)
@@ -334,7 +334,6 @@
     vmem = pl.BlockSpec(memory_space=pltpu.VMEM)
     dma = pltpu.SemaphoreType.DMA
     slots = far * NEAR
-    room = 12 * 2**20 + slots * 2 * all_heads * tokens * dim * 3
     out, tout = pl.pallas_call(
         functools.partial(kernel, far, hds),
         name="joint_attention",
@@ -342,7 +341,7 @@
             jax.ShapeDtypeStruct((groups, heads, tokens, dim), jnp.bfloat16),
             jax.ShapeDtypeStruct((PAIR, heads, share, dim), jnp.bfloat16),
         ),
-        in_specs=[pl.BlockSpec(memory_space=pltpu.HBM)] * 9 + [pl.BlockSpec(memory_space=pltpu.SMEM)],
+        in_specs=[pl.BlockSpec(memory_space=pl.ANY)] * 9 + [pl.BlockSpec(memory_space=pltpu.SMEM)],
         out_specs=(vmem, vmem),
         scratch_shapes=[
             pltpu.VMEM(positions.shape, jnp.int32),
@@ -374,7 +373,7 @@
             dma((2, heads)),
         ],
         compiler_params=pltpu.CompilerParams(
-            collective_id=0, has_side_effects=True, vmem_limit_bytes=room
+            collective_id=0, has_side_effects=True, vmem_limit_bytes=60 * 1024 * 1024
         ),
     )(
         by_head(video_q), by_head(video_k), by_head(video_v),

time: 47.6 us -> 42.3 us (0.89)
  local copies, waits for them, and re-layouts: 7.19 us -> 1.72 us
    unnamed x18 -> x4, local copies, waits for them, and re-layouts: 7.19 us -> 1.72 us
where the time goes in v5:
time: 42.3 us; the launch traced here: 42.1 us
  Pallas kernels  39.1 us (92%)
  local copies, waits for them, and re-layouts  1.72 us (4%)
  between operations  1.3 us (3%)
    pallas_call x1, Pallas kernels, local(): pl.pallas_call(functools.partial(kernel, far, hds), name='joint_attention...  38.4 us
    unnamed x4, local copies, waits for them, and re-layouts  1.72 us

profile of v5, /device:TPU:0, one launch (start us, length us, event | category | flops | bytes accessed | tf_op | source)
XLA Modules:
  0.0 42.1 jit_solution(12931236301300069522)
XLA Ops:
  1.3 38.4 %joint_attention.1 = (bf16[4,3,64,128]{3,2,1,0:T(8,128)(2,1)}, bf16[2,3,32,128]{3,2,1,0:T(8,128)(2,1)}) custom-call(bf16[4,3,64,128]{3,2,1,0:T(8,128)(2,1)} %bitcast.23, bf16[4,3,64,128]{3,2,1,0:T(8,128)(2,1)} %bitcast.24, bf16[4,3,64,128]{3,2,1,0:T(8,128)(2,1)} %bitcast.25, bf16[6,8,32,128]{3,2,1,0:T(8,128)(2,1)} %bitcast.20, ...), custom_call_target="tpu_custom_call" | custom-call | tf_op jit(solution)/shard_map/joint_attention/pallas_call | solution.py:337
  39.7 0.0 copy-start
  39.7 0.9 %copy-done = bf16[4,3,64,128]{3,2,1,0:T(8,128)(2,1)S(1)} copy-done((bf16[4,3,64,128]{3,2,1,0:T(8,128)(2,1)S(1)}, bf16[4,3,64,128]{3,2,1,0:T(8,128)(2,1)}, u32[]{:S(2)}) %copy-start) | copy-done | bytes 196632
  40.6 0.0 copy-start.1
  40.6 0.8 %copy-done.1 = bf16[2,3,32,128]{3,2,1,0:T(8,128)(2,1)S(1)} copy-done((bf16[2,3,32,128]{3,2,1,0:T(8,128)(2,1)S(1)}, bf16[2,3,32,128]{3,2,1,0:T(8,128)(2,1)}, u32[]{:S(2)}) %copy-start.1) | copy-done | bytes 49176
  41.4 0.7 %settle.1 = (bf16[4,3,64,128]{3,2,1,0:T(8,128)(2,1)}, bf16[2,3,32,128]{3,2,1,0:T(8,128)(2,1)}) custom-call(bf16[4,3,64,128]{3,2,1,0:T(8,128)(2,1)S(1)} %copy-done, bf16[2,3,32,128]{3,2,1,0:T(8,128)(2,1)S(1)} %copy-done.1), custom_call_target="tpu_custom_call" | custom-call | tf_op jit(solution)/shard_map/settle/pallas_call | solution.py:383
Async XLA Ops:
  39.7 0.9 %copy-start = (bf16[4,3,64,128]{3,2,1,0:T(8,128)(2,1)S(1)}, bf16[4,3,64,128]{3,2,1,0:T(8,128)(2,1)}, u32[]{:S(2)}) copy-start(bf16[4,3,64,128]{3,2,1,0:T(8,128)(2,1)} %get-tuple-element.6.out_ref) | copy-start | bytes 589828
  40.6 0.8 %copy-start.1 = (bf16[2,3,32,128]{3,2,1,0:T(8,128)(2,1)S(1)}, bf16[2,3,32,128]{3,2,1,0:T(8,128)(2,1)}, u32[]{:S(2)}) copy-start(bf16[2,3,32,128]{3,2,1,0:T(8,128)(2,1)} %get-tuple-element.7.tout_ref) | copy-start | bytes 147460

commit v6 on v5

--- a/solution.py
+++ b/solution.py
@@ -168,10 +168,10 @@
 
     for w, d in (early + late)[2:]:
         kv_to_group(w, d).start()
+    for d in straight_first + rest:
+        q_to_group(d).start()
     for w in range(2):
         spread(w, mine)
-    for d in straight_first + rest:
-        q_to_group(d).start()
     for w, d in (early + late)[2:]:
         g = group_of(d)
         arrived(slot, w, g)
@@ -262,13 +262,13 @@
     take(near_slot, 0)
     take(near_slot, 1)
     absorb(near_slot)
+    for w, d in late:
+        relay(last, w, d)
     take(across, 0)
     for h in range(heads):
         p, factor = weigh(h, jnp.concatenate([keys_of(straight, h), keys_of(across, h)], axis=0))
         probs[h] = p
         acc[h] = acc[h] * factor
-    for w, d in late:
-        relay(last, w, d)
     for h in range(heads):
         acc[h] += jnp.dot(probs[h, :, :rows], values_of(straight, h), preferred_element_type=jnp.float32)
     take(across, 1)

time: 42.3 us -> 40.2 us (0.950)
  Pallas kernels: 39.1 us -> 36.9 us
    pallas_call x1, Pallas kernels: 38.4 us -> 36.2 us  [local(): pl.pallas_call(functools.partial(kernel, far, hds), name='joint_attention...]
where the time goes in v6:
time: 40.2 us; the launch traced here: 40 us
  Pallas kernels  36.9 us (92%)
  local copies, waits for them, and re-layouts  1.72 us (4%)
  between operations  1.3 us (3%)
    pallas_call x1, Pallas kernels, local(): pl.pallas_call(functools.partial(kernel, far, hds), name='joint_attention...  36.2 us
    unnamed x4, local copies, waits for them, and re-layouts  1.72 us

profile of v6, /device:TPU:0, one launch (start us, length us, event | category | flops | bytes accessed | tf_op | source)
XLA Modules:
  0.0 40.0 jit_solution(3168289819370408485)
XLA Ops:
  1.3 36.2 %joint_attention.1 = (bf16[4,3,64,128]{3,2,1,0:T(8,128)(2,1)}, bf16[2,3,32,128]{3,2,1,0:T(8,128)(2,1)}) custom-call(bf16[4,3,64,128]{3,2,1,0:T(8,128)(2,1)} %bitcast.23, bf16[4,3,64,128]{3,2,1,0:T(8,128)(2,1)} %bitcast.24, bf16[4,3,64,128]{3,2,1,0:T(8,128)(2,1)} %bitcast.25, bf16[6,8,32,128]{3,2,1,0:T(8,128)(2,1)} %bitcast.20, ...), custom_call_target="tpu_custom_call" | custom-call | tf_op jit(solution)/shard_map/joint_attention/pallas_call | solution.py:337
  37.5 0.0 copy-start
  37.5 0.9 %copy-done = bf16[4,3,64,128]{3,2,1,0:T(8,128)(2,1)S(1)} copy-done((bf16[4,3,64,128]{3,2,1,0:T(8,128)(2,1)S(1)}, bf16[4,3,64,128]{3,2,1,0:T(8,128)(2,1)}, u32[]{:S(2)}) %copy-start) | copy-done | bytes 196632
  38.5 0.0 copy-start.1
  38.5 0.8 %copy-done.1 = bf16[2,3,32,128]{3,2,1,0:T(8,128)(2,1)S(1)} copy-done((bf16[2,3,32,128]{3,2,1,0:T(8,128)(2,1)S(1)}, bf16[2,3,32,128]{3,2,1,0:T(8,128)(2,1)}, u32[]{:S(2)}) %copy-start.1) | copy-done | bytes 49176
  39.3 0.7 %settle.1 = (bf16[4,3,64,128]{3,2,1,0:T(8,128)(2,1)}, bf16[2,3,32,128]{3,2,1,0:T(8,128)(2,1)}) custom-call(bf16[4,3,64,128]{3,2,1,0:T(8,128)(2,1)S(1)} %copy-done, bf16[2,3,32,128]{3,2,1,0:T(8,128)(2,1)S(1)} %copy-done.1), custom_call_target="tpu_custom_call" | custom-call | tf_op jit(solution)/shard_map/settle/pallas_call | solution.py:383
Async XLA Ops:
  37.5 0.9 %copy-start = (bf16[4,3,64,128]{3,2,1,0:T(8,128)(2,1)S(1)}, bf16[4,3,64,128]{3,2,1,0:T(8,128)(2,1)}, u32[]{:S(2)}) copy-start(bf16[4,3,64,128]{3,2,1,0:T(8,128)(2,1)} %get-tuple-element.6.out_ref) | copy-start | bytes 589828
  38.5 0.8 %copy-start.1 = (bf16[2,3,32,128]{3,2,1,0:T(8,128)(2,1)S(1)}, bf16[2,3,32,128]{3,2,1,0:T(8,128)(2,1)}, u32[]{:S(2)}) copy-start(bf16[2,3,32,128]{3,2,1,0:T(8,128)(2,1)} %get-tuple-element.7.tout_ref) | copy-start | bytes 147460

commit v7 on v6

--- a/solution.py
+++ b/solution.py
@@ -386,7 +386,6 @@
         out_shape=(jax.ShapeDtypeStruct(out.shape, out.dtype), jax.ShapeDtypeStruct(tout.shape, tout.dtype)),
         in_specs=[vmem] * 2,
         out_specs=(vmem, vmem),
-        compiler_params=pltpu.CompilerParams(vmem_limit_bytes=4 * 2**20),
     )(out, tout)
     video_out = jnp.swapaxes(out.reshape(all_heads, tokens, dim), 0, 1)
     text_out = jnp.swapaxes(tout.reshape(PAIR * heads, share, dim), 0, 1)

time: 40.2 us -> 39.3 us (0.978)
  local copies, waits for them, and re-layouts: 1.72 us -> 0 us
  Pallas kernels: 36.9 us -> 37.9 us
    unnamed x4 -> x0, local copies, waits for them, and re-layouts: 1.72 us -> none
    pallas_call x1, Pallas kernels: 0.7 us -> 1.63 us  [local(): pl.pallas_call(settle, name='settle', out_shape=(jax.ShapeDtypeStruct(out...]
where the time goes in v7:
time: 39.3 us; the launch traced here: 39.2 us
  Pallas kernels  37.9 us (96%)
  between operations  1.29 us (3%)
    pallas_call x1, Pallas kernels, local(): pl.pallas_call(functools.partial(kernel, far, hds), name='joint_attention...  36.3 us
    pallas_call x1, Pallas kernels, local(): pl.pallas_call(settle, name='settle', out_shape=(jax.ShapeDtypeStruct(out...  1.63 us

profile of v7, /device:TPU:0, one launch (start us, length us, event | category | flops | bytes accessed | tf_op | source)
XLA Modules:
  0.0 39.2 jit_solution(1462085521555080010)
XLA Ops:
  1.3 36.3 %joint_attention.1 = (bf16[4,3,64,128]{3,2,1,0:T(8,128)(2,1)}, bf16[2,3,32,128]{3,2,1,0:T(8,128)(2,1)}) custom-call(bf16[4,3,64,128]{3,2,1,0:T(8,128)(2,1)} %bitcast.23, bf16[4,3,64,128]{3,2,1,0:T(8,128)(2,1)} %bitcast.24, bf16[4,3,64,128]{3,2,1,0:T(8,128)(2,1)} %bitcast.25, bf16[6,8,32,128]{3,2,1,0:T(8,128)(2,1)} %bitcast.20, ...), custom_call_target="tpu_custom_call" | custom-call | tf_op jit(solution)/shard_map/joint_attention/pallas_call | solution.py:337
  37.5 1.6 %settle.1 = (bf16[4,3,64,128]{3,2,1,0:T(8,128)(2,1)}, bf16[2,3,32,128]{3,2,1,0:T(8,128)(2,1)}) custom-call(bf16[4,3,64,128]{3,2,1,0:T(8,128)(2,1)} %get-tuple-element.6.out_ref, bf16[2,3,32,128]{3,2,1,0:T(8,128)(2,1)} %get-tuple-element.7.tout_ref), custom_call_target="tpu_custom_call" | custom-call | tf_op jit(solution)/shard_map/settle/pallas_call | solution.py:383
